TPU v7x, 256 devices: a whole 4x4x8 slice. The times are simulated.
256 devices in a mesh: row: 16 (over x_lo, y, core), col: 16 (over z, x_hi).
Axes of the slice: x: 4 (x_hi: 2, x_lo: 2; x = x_hi * 2 + x_lo), y: 4, z: 8, core: 2. Of those that a mesh axis runs over, the one named last changes fastest.
Arguments:
- block_vecs: float32 [16, 131072], P(None, ('col', 'row')), may hold values from -130 to 130
- direction: float32 [16, 131072], P(None, ('col', 'row')), may hold values from -130 to 130
- blocks: bfloat16 [1024, 32, 128, 128], P('col', 'row'), may hold values from 0 to 4
- block_cols: int32 [1024, 32], P('col', 'row'), may hold values from 0 to 1023, as said below
- live_counts: int32 [1024, 16], P('col', 'row'), may hold values from 1 to 2, as said below
Outputs:
- x_next: float32 [16, 131072], P(None, ('col', 'row'))
- reduced: float32 [48, 48], replicated
- residual: float32 [16, 131072], P(None, ('col', 'row'))
Inputs may be any that keep to these rules, and one draw needn't show every extreme that they name: `block_cols`: A block column index g in slots 2 * r to 2 * r + 1 of any block row satisfies (g // 4) mod 16 == r. `live_counts`: every block row has 2 live slots in at least one segment.
All inputs are finite; a program needn't handle non-finite values.
Results may differ from a plain program's by a relative error of at most 0.0003.
Values sent between devices are 32-bit elements; how exact they have to be, the bound alone decides.
A program may use at most 64 MiB of HBM per device.

v0:
```python
import math
import jax
import jax.numpy as jnp
from jax import lax
from jax.sharding import PartitionSpec as P

highest = lax.Precision.HIGHEST


def outer(left, right):
    return jnp.dot(left, right.T, precision=highest, preferred_element_type=jnp.float32)


def cholesky_lower(matrix):
    order_small = matrix.shape[0]
    places = jnp.arange(order_small, dtype=jnp.int32)

    def column_step(step, lower):
        pick = (places == step).astype(jnp.float32)
        row_now = jnp.sum(lower * pick[:, None], axis=0)
        column_now = jnp.sum(matrix * pick[None, :], axis=1)
        pivot = jnp.sum(column_now * pick) - jnp.sum(row_now * row_now)
        pivot_root = jnp.sqrt(pivot)
        below = (column_now - jnp.sum(lower * row_now[None, :], axis=1)) / pivot_root
        values = jnp.where(places > step, below, jnp.where(places == step, pivot_root, 0.0))
        return lower + values[:, None] * pick[None, :]

    return lax.fori_loop(0, order_small, column_step, jnp.zeros_like(matrix))


def solve_lower(lower, right):
    order_small = lower.shape[0]
    places = jnp.arange(order_small, dtype=jnp.int32)

    def row_step(step, solved):
        pick = (places == step).astype(jnp.float32)
        row_now = jnp.sum(lower * pick[:, None], axis=0)
        pivot = jnp.sum(row_now * pick)
        right_row = jnp.sum(right * pick[:, None], axis=0)
        value = (right_row - jnp.sum(row_now[:, None] * solved, axis=0)) / pivot
        return solved + pick[:, None] * value[None, :]

    return lax.fori_loop(0, order_small, row_step, jnp.zeros_like(right))


def solve_upper_t(lower, right):
    order_small = lower.shape[0]
    places = jnp.arange(order_small, dtype=jnp.int32)

    def row_step(count, solved):
        step = order_small - 1 - count
        pick = (places == step).astype(jnp.float32)
        column_now = jnp.sum(lower * pick[None, :], axis=1)
        pivot = jnp.sum(column_now * pick)
        right_row = jnp.sum(right * pick[:, None], axis=0)
        value = (right_row - jnp.sum(column_now[:, None] * solved, axis=0)) / pivot
        return solved + pick[:, None] * value[None, :]

    return lax.fori_loop(0, order_small, row_step, jnp.zeros_like(right))


def local_layout(block_cols, live_counts, span_rows, block_size, row_count):
    per_span = span_rows // block_size
    span_index = block_cols // per_span
    local_cols = span_index // row_count * per_span + block_cols % per_span
    slot_count = block_cols.shape[1]
    live_mask = (jnp.arange(slot_count, dtype=jnp.int32)[None, :] < live_counts).astype(jnp.float32)
    return (local_cols, live_mask)


def forward_part(col_panel, blocks, local_cols, live_mask):
    vec_width = col_panel.shape[0]
    block_size = blocks.shape[2]
    col_blocks = col_panel.reshape(vec_width, -1, block_size)
    picked = col_blocks[:, local_cols, :] * live_mask[None, :, :, None]
    forward = jnp.einsum(
        "vbkj,bkij->vbi", picked, blocks, precision=highest, preferred_element_type=jnp.float32
    )
    return 0.5 * forward.reshape(vec_width, -1)


def backward_part(row_panel, col_length, blocks, local_cols, live_mask):
    vec_width = row_panel.shape[0]
    block_size = blocks.shape[2]
    row_blocks = row_panel.reshape(vec_width, -1, block_size)
    backward = (
        jnp.einsum(
            "vbi,bkij->vbkj",
            row_blocks,
            blocks,
            precision=highest,
            preferred_element_type=jnp.float32,
        )
        * live_mask[None, :, :, None]
    )
    spread = jnp.zeros((vec_width, col_length // block_size, block_size), jnp.float32)
    spread = spread.at[:, local_cols.reshape(-1), :].add(
        backward.reshape(vec_width, -1, block_size)
    )
    return 0.5 * spread.reshape(vec_width, -1)


def per_device(block_vecs, direction, blocks, block_cols, live_counts):
    row_count = lax.axis_size("row")
    col_count = lax.axis_size("col")
    vec_width = block_vecs.shape[0]
    span_rows = block_vecs.shape[1]
    order_total = span_rows * row_count * col_count
    col_length = span_rows * col_count
    block_size = blocks.shape[2]
    local_cols, live_mask = local_layout(block_cols, live_counts, span_rows, block_size, row_count)
    paired = jnp.concatenate([block_vecs, direction], axis=0)
    pair_cols = lax.all_gather(paired, "col", axis=1, tiled=True)
    pair_rows = lax.all_gather(paired, "row", axis=1, tiled=True)
    forward = forward_part(pair_cols, blocks, local_cols, live_mask)
    backward = backward_part(pair_rows, col_length, blocks, local_cols, live_mask)
    image_pair = lax.psum_scatter(
        forward, "row", scatter_dimension=1, tiled=True
    ) + lax.psum_scatter(backward, "col", scatter_dimension=1, tiled=True)
    image_x = image_pair[:vec_width]
    image_p = image_pair[vec_width:]
    gram_x, cross_x = lax.psum(
        (outer(block_vecs, block_vecs), outer(block_vecs, image_x)), ("row", "col")
    )
    factor_x = cholesky_lower(gram_x)
    coefficient = solve_upper_t(factor_x, solve_lower(factor_x, cross_x))
    resid = image_x - jnp.dot(
        coefficient.T, block_vecs, precision=highest, preferred_element_type=jnp.float32
    )
    basis = jnp.concatenate([block_vecs, resid, direction], axis=0)
    resid_cols = lax.all_gather(resid, "col", axis=1, tiled=True)
    resid_rows = lax.all_gather(resid, "row", axis=1, tiled=True)
    forward_r = forward_part(resid_cols, blocks, local_cols, live_mask)
    column_x = outer(basis, image_x)
    column_p = outer(basis, image_p)
    backward_r = backward_part(resid_rows, col_length, blocks, local_cols, live_mask)
    image_r = lax.psum_scatter(
        forward_r, "row", scatter_dimension=1, tiled=True
    ) + lax.psum_scatter(backward_r, "col", scatter_dimension=1, tiled=True)
    column_r = outer(basis, image_r)
    gram_apply = jnp.concatenate([column_x, column_r, column_p], axis=1)
    gram_basis, gram_apply = lax.psum((outer(basis, basis), gram_apply), ("row", "col"))
    factor = cholesky_lower(gram_basis)
    halfway = solve_lower(factor, 0.5 * (gram_apply + gram_apply.T))
    reduced = solve_lower(factor, halfway.T)
    shifted = reduced + 3.0 * jnp.eye(3 * vec_width, dtype=jnp.float32)
    target = jnp.dot(
        shifted, shifted[:, :vec_width], precision=highest, preferred_element_type=jnp.float32
    )
    mixing = solve_upper_t(factor, target)
    fresh = jnp.dot(mixing.T, basis, precision=highest, preferred_element_type=jnp.float32)
    gram_fresh = lax.psum(outer(fresh, fresh), ("row", "col"))
    factor_fresh = cholesky_lower(gram_fresh)
    x_next = math.sqrt(order_total) * solve_lower(factor_fresh, fresh)
    return (x_next, reduced, resid)


def solution(mesh):
    return jax.shard_map(
        per_device,
        mesh=mesh,
        in_specs=(
            P(None, ("col", "row")),
            P(None, ("col", "row")),
            P("col", "row", None, None),
            P("col", "row"),
            P("col", "row"),
        ),
        out_specs=(P(None, ("col", "row")), P(), P(None, ("col", "row"))),
        check_vma=False,
    )
```

profile of v0, /device:TPU:1, one launch (start us, length us, event | category | flops | bytes accessed | tf_op | source)
XLA Modules:
  0.0 1421.3 jit_solution(11187509048310806808)
XLA Ops:
  7.2 0.8 constant_dynamic-update-slice_fusion.1
  8.0 0.8 constant_dynamic-update-slice_fusion
  9.4 0.7 all-gather.3.cloned.1.call-update
  10.2 0.7 fusion.60
  10.9 0.7 compare_select_fusion.9
  11.9 37.2 %all-gather.5.cloned.1.call-done = f32[32,8192]{1,0:T(8,128)} async-done(((f32[32,512]{1,0:T(8,128)}), f32[32,8192]{1,0:T(8,128)}) %all-gather.5.cloned.1.call-update) | async-done | bytes 1048592 | tf_op jit(solution)/shard_map/all_gather | solution.py:114
  49.0 1.4 copy.57
  50.4 4.3 convolution_multiply_fusion
  54.9 5.7 scatter_fusion
  60.6 1.1 copy_bitcast_fusion
  62.0 64.4 %all-gather.3.cloned.1.call-done = f32[32,8192]{1,0:T(8,128)} async-done(((f32[32,512]{1,0:T(8,128)}), f32[32,8192]{1,0:T(8,128)}) %all-gather.3.cloned.1.call-update) | async-done | bytes 1048592 | tf_op jit(solution)/shard_map/all_gather | solution.py:113
  126.4 1.4 copy_bitcast_fusion.2
  127.8 0.8 gather_fusion
  128.6 6.0 fusion.45
  134.6 1.1 copy.69
  135.9 192.4 %reduce-scatter.7.cloned.1.call-done = f32[32,512]{1,0:T(8,128)} async-done(((f32[32,8192]{1,0:T(8,128)}), f32[32,512]{1,0:T(8,128)}) %reduce-scatter.7.cloned.1.call-update) | async-done | bytes 65552 | tf_op jit(solution)/shard_map/reduce_scatter | solution.py:119
  328.3 66.4 %reduce-scatter.5.cloned.1.call-done = f32[32,512]{1,0:T(8,128)} async-done(((f32[32,8192]{1,0:T(8,128)}), f32[32,512]{1,0:T(8,128)}) %reduce-scatter.5.cloned.1.call-update) | async-done | bytes 65552 | tf_op jit(solution)/shard_map/reduce_scatter | solution.py:117
  394.7 0.9 add.271
  395.7 78.8 %all-reduce.1 = (f32[16,16]{0,1:T(8,128)S(1)}, f32[16,16]{1,0:T(8,128)S(1)}) all-reduce(f32[16,16]{0,1:T(8,128)S(1)} %convolution_bitcast_fusion.1, f32[16,16]{1,0:T(8,128)S(1)} %fusion.72), channel_id=1, replica_groups=mesh['row'=16,'col'=16] {'row','col'}, use_global_device_ids=true, to_apply=%region_11.12 | all-reduce | flops 512 | bytes 4096 | tf_op jit(solution)/shard_map/psum | solution.py:122
  474.5 37.0 %while.135 = (s32[]{:T(128)}, f32[16,16]{1,0:T(8,128)S(1)}, f32[16,16]{1,0:T(8,128)S(1)}, s32[]{:T(128)}, s32[]{:T(128)}) while((s32[]{:T(128)}, f32[16,16]{1,0:T(8,128)S(1)}, f32[16,16]{1,0:T(8,128)S(1)}, s32[]{:T(128)}, s32[]{:T(128)}) %tuple.302), condition=%wide.region_10.11_spmd.clone.clone, body=%wide.region_4.10_spmd.clone.clone.sunk | while | flops 2978 | bytes 6069 | solution.py:28
  511.6 24.3 %while.129 = (s32[]{:T(128)}, f32[16,16]{1,0:T(8,128)S(1)}, f32[16,16]{1,0:T(8,128)S(1)}, f32[16,16]{1,0:T(8,128)S(1)}, s32[]{:T(128)}, /*index=5*/s32[]{:T(128)}) while((s32[]{:T(128)}, f32[16,16]{1,0:T(8,128)S(1)}, f32[16,16]{1,0:T(8,128)S(1)}, f32[16,16]{1,0:T(8,128)S(1)}, s32[]{:T(128)}, /*index=5*/s32[]{:T(128)}) %tuple.305), condition=%wide.region_17.18_spmd.clone, body=%wide.region_12.17_spmd.clone.sunk | while | flops 2626 | bytes 5984 | solution.py:43
  535.9 24.8 %while.130 = (s32[]{:T(128)}, f32[16,16]{1,0:T(8,128)S(1)}, f32[16,16]{1,0:T(8,128)S(1)}, f32[16,16]{1,0:T(8,128)S(1)}, s32[]{:T(128)}, /*index=5*/s32[]{:T(128)}, s32[]{:T(128)}) while((s32[]{:T(128)}, f32[16,16]{1,0:T(8,128)S(1)}, f32[16,16]{1,0:T(8,128)S(1)}, f32[16,16]{1,0:T(8,128)S(1)}, s32[]{:T(128)}, ...), condition=%wide.region_23.24_spmd.clone, body=%wide.region_18.23_spmd.clone.sunk | while | flops 2627 | bytes 6004 | solution.py:59
  560.9 19.6 %all_gather.15 = f32[16,8192]{1,0:T(8,128)S(1)} all-gather(f32[16,512]{1,0:T(8,128)S(1)} %convolution_subtract_fusion), channel_id=1, replica_groups=mesh['row'=16,'col'=16] {'row'}, dimensions={1}, use_global_device_ids=true | all-gather | bytes 557056 | tf_op jit(solution)/shard_map/all_gather | solution.py:132
  580.6 3.8 convolution_multiply_fusion.1
  584.5 5.2 scatter_fusion.1
  589.7 0.8 copy_bitcast_fusion.3
  590.6 34.6 %all_gather.14 = f32[16,8192]{1,0:T(8,128)S(1)} all-gather(f32[16,512]{1,0:T(8,128)S(1)} %convolution_subtract_fusion), channel_id=1, replica_groups=mesh['row'=16,'col'=16] {'col'}, dimensions={1}, use_global_device_ids=true | all-gather | bytes 557056 | tf_op jit(solution)/shard_map/all_gather | solution.py:131
  625.3 0.8 gather_fusion.1
  626.0 5.2 fusion.49
  631.2 0.8 copy.70
  632.8 145.4 %reduce-scatter.11.cloned.1.call-done = f32[16,512]{1,0:T(8,128)} async-done(((f32[16,8192]{1,0:T(8,128)}), f32[16,512]{1,0:T(8,128)}) %reduce-scatter.11.cloned.1.call-update) | async-done | bytes 32784 | tf_op jit(solution)/shard_map/reduce_scatter | solution.py:139
  778.1 65.7 %reduce-scatter.9.cloned.1.call-done = f32[16,512]{1,0:T(8,128)} async-done(((f32[16,8192]{1,0:T(8,128)}), f32[16,512]{1,0:T(8,128)}) %reduce-scatter.9.cloned.1.call-update) | async-done | bytes 32784 | tf_op jit(solution)/shard_map/reduce_scatter | solution.py:137
  843.8 0.9 fusion.58
  844.8 79.4 %all-reduce = (f32[48,48]{0,1:T(8,128)S(1)}, f32[48,48]{1,0:T(8,128)S(1)}) all-reduce(f32[48,48]{0,1:T(8,128)S(1)} %pad_maximum_fusion.1, f32[48,48]{1,0:T(8,128)S(1)} %fusion.70), channel_id=1, replica_groups=mesh['row'=16,'col'=16] {'row','col'}, use_global_device_ids=true, to_apply=%region_35.36 | all-reduce | flops 4608 | bytes 36864 | tf_op jit(solution)/shard_map/psum | solution.py:142
  924.3 111.3 %while.136 = (s32[]{:T(128)}, f32[48,48]{1,0:T(8,128)S(1)}, f32[48,48]{1,0:T(8,128)S(1)}, s32[]{:T(128)}, s32[]{:T(128)}) while((s32[]{:T(128)}, f32[48,48]{1,0:T(8,128)S(1)}, f32[48,48]{1,0:T(8,128)S(1)}, s32[]{:T(128)}, s32[]{:T(128)}) %tuple.311), condition=%wide.region_31.32_spmd.clone.clone, body=%wide.region_25.31_spmd.clone.clone.sunk | while | flops 25826 | bytes 48693 | solution.py:28
  1035.6 79.4 %while.131 = (s32[]{:T(128)}, f32[48,48]{1,0:T(8,128)S(1)}, f32[48,48]{1,0:T(8,128)S(1)}, f32[48,48]{1,0:T(8,128)S(1)}, s32[]{:T(128)}, /*index=5*/s32[]{:T(128)}) while((s32[]{:T(128)}, f32[48,48]{1,0:T(8,128)S(1)}, f32[48,48]{1,0:T(8,128)S(1)}, f32[48,48]{1,0:T(8,128)S(1)}, s32[]{:T(128)}, /*index=5*/s32[]{:T(128)}) %tuple.314), condition=%wide.region_41.42_spmd.clone, body=%wide.region_36.41_spmd.clone.sunk | while | flops 23234 | bytes 48480 | solution.py:43
  1038.1 0.7 subtract_divide_fusion.14
  1048.1 0.7 subtract_divide_fusion.14
  1049.7 0.7 subtract_divide_fusion.14
  1058.0 0.7 subtract_divide_fusion.14
  1059.6 0.7 subtract_divide_fusion.14
  1069.6 0.7 subtract_divide_fusion.14
  1079.5 0.7 subtract_divide_fusion.14
  1115.1 79.4 %while.132 = (s32[]{:T(128)}, f32[48,48]{1,0:T(8,128)S(1)}, f32[48,48]{1,0:T(8,128)S(1)}, f32[48,48]{1,0:T(8,128)S(1)}, s32[]{:T(128)}, /*index=5*/s32[]{:T(128)}) while((s32[]{:T(128)}, f32[48,48]{1,0:T(8,128)S(1)}, f32[48,48]{1,0:T(8,128)S(1)}, f32[48,48]{1,0:T(8,128)S(1)}, s32[]{:T(128)}, /*index=5*/s32[]{:T(128)}) %tuple.344), condition=%wide.region_47.48_spmd.clone, body=%wide.region_42.47_spmd.clone.sunk | while | flops 23234 | bytes 48480 | solution.py:43
  1194.8 81.8 %while.133 = (s32[]{:T(128)}, f32[48,16]{0,1:T(8,128)S(1)}, f32[48,16]{0,1:T(8,128)S(1)}, f32[48,48]{1,0:T(8,128)S(1)}, s32[]{:T(128)}, /*index=5*/s32[]{:T(128)}, s32[]{:T(128)}) while((s32[]{:T(128)}, f32[48,16]{0,1:T(8,128)S(1)}, f32[48,16]{0,1:T(8,128)S(1)}, f32[48,48]{1,0:T(8,128)S(1)}, s32[]{:T(128)}, ...), condition=%wide.region_53.54_spmd.clone, body=%wide.region_48.53_spmd.clone.sunk | while | flops 10947 | bytes 23348 | solution.py:59
  1276.8 73.6 %psum.39 = f32[16,16]{1,0:T(8,128)S(1)} all-reduce(f32[16,16]{1,0:T(8,128)S(1)} %fusion.73), channel_id=1, replica_groups=mesh['row'=16,'col'=16] {'row','col'}, use_global_device_ids=true, to_apply=%region_54.55 | all-reduce | flops 256 | bytes 2048 | tf_op jit(solution)/shard_map/psum | solution.py:152
  1350.5 37.0 %while.137 = (s32[]{:T(128)}, f32[16,16]{1,0:T(8,128)S(1)}, f32[16,16]{1,0:T(8,128)S(1)}, s32[]{:T(128)}, s32[]{:T(128)}) while((s32[]{:T(128)}, f32[16,16]{1,0:T(8,128)S(1)}, f32[16,16]{1,0:T(8,128)S(1)}, s32[]{:T(128)}, s32[]{:T(128)}) %tuple.323), condition=%wide.region_61.62_spmd.clone.clone, body=%wide.region_55.61_spmd.clone.clone.sunk | while | flops 2978 | bytes 6069 | solution.py:28
  1387.5 26.3 %while.134 = (s32[]{:T(128)}, f32[16,512]{1,0:T(8,128)S(1)}, f32[16,512]{1,0:T(8,128)S(1)}, f32[16,16]{1,0:T(8,128)S(1)}, s32[]{:T(128)}, /*index=5*/s32[]{:T(128)}) while((s32[]{:T(128)}, f32[16,512]{1,0:T(8,128)S(1)}, f32[16,512]{1,0:T(8,128)S(1)}, f32[16,16]{1,0:T(8,128)S(1)}, s32[]{:T(128)}, /*index=5*/s32[]{:T(128)}) %tuple.326), condition=%wide.region_67.68_spmd.clone, body=%wide.region_62.67_spmd.clone.sunk | while | flops 66114 | bytes 144928 | solution.py:43
  (1682 shorter events, 393.6 us)
Async XLA Ops:
  7.2 41.9 %all-gather.5.cloned.1.call-start = ((), (), s32[]{:S(2)}) async-start(), calls=%async_computation.6 | async-start | bytes 1114112 | tf_op jit(solution)/shard_map/all_gather | solution.py:114
  8.7 0.6 copy-start.4
  9.4 117.1 %all-gather.3.cloned.1.call-start = ((), (), s32[]{:S(2)}) async-start(), calls=%async_computation.4 | async-start | bytes 1114112 | tf_op jit(solution)/shard_map/all_gather | solution.py:113
  10.1 318.2 %reduce-scatter.7.cloned.1.call-start = ((), (), s32[]{:S(2)}) async-start(), calls=%async_computation.7 | async-start | bytes 1114112 | tf_op jit(solution)/shard_map/reduce_scatter | solution.py:119
  61.7 333.0 %reduce-scatter.5.cloned.1.call-start = ((), (), s32[]{:S(2)}) async-start(), calls=%async_computation.5 | async-start | bytes 1114112 | tf_op jit(solution)/shard_map/reduce_scatter | solution.py:117
  134.6 1.2 copy-start.1
  135.7 642.4 %reduce-scatter.11.cloned.1.call-start = ((), (), s32[]{:S(2)}) async-start(), calls=%async_computation.9 | async-start | bytes 557056 | tf_op jit(solution)/shard_map/reduce_scatter | solution.py:139
  560.9 715.6 %copy-start.2 = (f32[16,512]{1,0:T(8,128)}, f32[16,512]{1,0:T(8,128)S(1)}, u32[]{:S(2)}) copy-start(f32[16,512]{1,0:T(8,128)S(1)} %convolution_subtract_fusion) | copy-start | bytes 98308
  590.5 253.3 %reduce-scatter.9.cloned.1.call-start = ((), (), s32[]{:S(2)}) async-start(), calls=%async_computation.8 | async-start | bytes 557056 | tf_op jit(solution)/shard_map/reduce_scatter | solution.py:137
  626.0 6.1 copy-start.3
  1194.5 219.9 %copy-start = (f32[48,48]{1,0:T(8,128)}, f32[48,48]{1,0:T(8,128)S(1)}, u32[]{:S(2)}) copy-start(f32[48,48]{1,0:T(8,128)S(1)} %get-tuple-element.811) | copy-start | bytes 27652
Sparse Core Ops, SparseCore 0:
  9.8 39.1 all-gather.4
  51.6 74.7 all-gather.2
  130.3 198.0 reduce-scatter.6
  330.7 63.9 reduce-scatter.4
  590.6 187.4 reduce-scatter.10
  780.5 63.2 reduce-scatter.8
where the time goes:
time: 1430 us; the launch traced here: 1420 us
  waiting for transfers between devices  572 us (40%)
  other arithmetic  410 us (29%)
  blocking collectives  286 us (20%)
  loops' own time  107 us (7%)
  matrix products  21.8 us (2%)
  between operations  14.4 us (1%)
    reduce_scatter x1, waiting for transfers between devices, per_device(): lax.psum_scatter(backward, 'col', scatter_dimension=1, tiled=True)  192 us
    reduce_scatter x1, waiting for transfers between devices, per_device(): lax.psum_scatter(backward_r, 'col', scatter_dimension=1, tiled=True)  145 us
    another operation x3, loops' own time, cholesky_lower(): return lax.fori_loop(0, order_small, column_step, jnp.zeros_like(matrix))  105 us
    div x128, other arithmetic, row_step(): value = (right_row - jnp.sum(row_now[:, None] * solved, axis=0)) / pivot  87.9 us
    reduce_sum x128, other arithmetic, row_step(): pivot = jnp.sum(row_now * pick)  85.7 us
    psum x1, blocking collectives, per_device(): lax.psum((outer(basis, basis), gram_apply), ('row', 'col'))  79.4 us
    psum x1, blocking collectives, per_device(): lax.psum((outer(block_vecs, block_vecs), outer(block_vecs, image_x)), ('r...  78.8 us
    psum x1, blocking collectives, per_device(): gram_fresh = lax.psum(outer(fresh, fresh), ('row', 'col'))  73.6 us
  transfers between devices with their start and end apart: 6, of which 6 were waited for; matrix products, arithmetic and copies ran while one was open for 2% of the time, Pallas kernels for 0%

commit v1 on v0

--- a/solution.py
+++ b/solution.py
@@ -101,6 +101,11 @@
 
 
 def per_device(block_vecs, direction, blocks, block_cols, live_counts):
+
+    def apply_positions_on(own_rows, link_axis, device_axis):
+        x_now = lax.psum(lax.psum(own_rows, link_axis), device_axis)
+        return x_now
+
     row_count = lax.axis_size("row")
     col_count = lax.axis_size("col")
     vec_width = block_vecs.shape[0]
@@ -119,8 +124,8 @@
     ) + lax.psum_scatter(backward, "col", scatter_dimension=1, tiled=True)
     image_x = image_pair[:vec_width]
     image_p = image_pair[vec_width:]
-    gram_x, cross_x = lax.psum(
-        (outer(block_vecs, block_vecs), outer(block_vecs, image_x)), ("row", "col")
+    gram_x, cross_x = apply_positions_on(
+        (outer(block_vecs, block_vecs), outer(block_vecs, image_x)), "col", "row"
     )
     factor_x = cholesky_lower(gram_x)
     coefficient = solve_upper_t(factor_x, solve_lower(factor_x, cross_x))

time: 1430 us -> 1480 us (1.035)
  blocking collectives: 286 us -> 337 us
    psum x1 -> x2, blocking collectives: 78.8 us -> 129 us  [apply_positions_on(): x_now = lax.psum(lax.psum(own_rows, link_axis), device_axis)]
where the time goes in v1:
time: 1480 us; the launch traced here: 1470 us
  waiting for transfers between devices  574 us (39%)
  other arithmetic  410 us (28%)
  blocking collectives  337 us (23%)
  loops' own time  107 us (7%)
  matrix products  21.8 us (1%)
    reduce_scatter x1, waiting for transfers between devices, per_device(): lax.psum_scatter(backward, 'col', scatter_dimension=1, tiled=True)  192 us
    reduce_scatter x1, waiting for transfers between devices, per_device(): lax.psum_scatter(backward_r, 'col', scatter_dimension=1, tiled=True)  147 us
    psum x2, blocking collectives, apply_positions_on(): x_now = lax.psum(lax.psum(own_rows, link_axis), device_axis)  129 us
    another operation x3, loops' own time, cholesky_lower(): return lax.fori_loop(0, order_small, column_step, jnp.zeros_like(matrix))  105 us
    div x128, other arithmetic, row_step(): value = (right_row - jnp.sum(row_now[:, None] * solved, axis=0)) / pivot  87.9 us
    reduce_sum x128, other arithmetic, row_step(): pivot = jnp.sum(row_now * pick)  85.7 us
    psum x1, blocking collectives, per_device(): lax.psum((outer(basis, basis), gram_apply), ('row', 'col'))  79.4 us
    psum x1, blocking collectives, per_device(): gram_fresh = lax.psum(outer(fresh, fresh), ('row', 'col'))  73.6 us
  transfers between devices with their start and end apart: 6, of which 6 were waited for; matrix products, arithmetic and copies ran while one was open for 2% of the time, Pallas kernels for 0%

profile of v1, /device:TPU:1, one launch (start us, length us, event | category | flops | bytes accessed | tf_op | source)
XLA Modules:
  0.0 1473.7 jit_solution(2716898674604223993)
XLA Ops:
  7.2 0.8 constant_dynamic-update-slice_fusion.1
  8.0 0.8 constant_dynamic-update-slice_fusion
  9.4 0.7 all-gather.3.cloned.1.call-update
  10.2 0.7 fusion.60
  10.9 0.7 compare_select_fusion.9
  11.9 37.2 %all-gather.5.cloned.1.call-done = f32[32,8192]{1,0:T(8,128)} async-done(((f32[32,512]{1,0:T(8,128)}), f32[32,8192]{1,0:T(8,128)}) %all-gather.5.cloned.1.call-update) | async-done | bytes 1048592 | tf_op jit(solution)/shard_map/all_gather | solution.py:119
  49.0 1.4 copy.57
  50.4 4.3 convolution_multiply_fusion
  54.9 5.7 scatter_fusion
  60.6 1.1 copy_bitcast_fusion
  62.0 64.4 %all-gather.3.cloned.1.call-done = f32[32,8192]{1,0:T(8,128)} async-done(((f32[32,512]{1,0:T(8,128)}), f32[32,8192]{1,0:T(8,128)}) %all-gather.3.cloned.1.call-update) | async-done | bytes 1048592 | tf_op jit(solution)/shard_map/all_gather | solution.py:118
  126.4 1.4 copy_bitcast_fusion.2
  127.8 0.8 gather_fusion
  128.6 6.0 fusion.45
  134.6 1.1 copy.69
  135.9 192.4 %reduce-scatter.7.cloned.1.call-done = f32[32,512]{1,0:T(8,128)} async-done(((f32[32,8192]{1,0:T(8,128)}), f32[32,512]{1,0:T(8,128)}) %reduce-scatter.7.cloned.1.call-update) | async-done | bytes 65552 | tf_op jit(solution)/shard_map/reduce_scatter | solution.py:124
  328.3 66.4 %reduce-scatter.5.cloned.1.call-done = f32[32,512]{1,0:T(8,128)} async-done(((f32[32,8192]{1,0:T(8,128)}), f32[32,512]{1,0:T(8,128)}) %reduce-scatter.5.cloned.1.call-update) | async-done | bytes 65552 | tf_op jit(solution)/shard_map/reduce_scatter | solution.py:122
  394.7 0.9 add.275
  395.7 63.1 %all-reduce.1 = (f32[16,16]{0,1:T(8,128)S(1)}, f32[16,16]{1,0:T(8,128)S(1)}) all-reduce(f32[16,16]{0,1:T(8,128)S(1)} %convolution_bitcast_fusion.1, f32[16,16]{1,0:T(8,128)S(1)} %fusion.72), channel_id=1, replica_groups=mesh['row'=16,'col'=16] {'col'}, use_global_device_ids=true, to_apply=%region_12.13 | all-reduce | flops 512 | bytes 4096 | tf_op jit(solution)/shard_map/psum | solution.py:106
  458.8 66.3 %all-reduce.2 = (f32[16,16]{0,1:T(8,128)S(1)}, f32[16,16]{1,0:T(8,128)S(1)}) all-reduce(f32[16,16]{0,1:T(8,128)S(1)} %get-tuple-element.1100, f32[16,16]{1,0:T(8,128)S(1)} %get-tuple-element.1101), channel_id=1, replica_groups=mesh['row'=16,'col'=16] {'row'}, use_global_device_ids=true, to_apply=%region_13.14 | all-reduce | flops 512 | bytes 4096 | tf_op jit(solution)/shard_map/psum | solution.py:106
  525.2 37.0 %while.135 = (s32[]{:T(128)}, f32[16,16]{1,0:T(8,128)S(1)}, f32[16,16]{1,0:T(8,128)S(1)}, s32[]{:T(128)}, s32[]{:T(128)}) while((s32[]{:T(128)}, f32[16,16]{1,0:T(8,128)S(1)}, f32[16,16]{1,0:T(8,128)S(1)}, s32[]{:T(128)}, s32[]{:T(128)}) %tuple.302), condition=%wide.region_11.12_spmd.clone.clone, body=%wide.region_5.11_spmd.clone.clone.sunk | while | flops 2978 | bytes 6069 | solution.py:28
  562.3 24.3 %while.129 = (s32[]{:T(128)}, f32[16,16]{1,0:T(8,128)S(1)}, f32[16,16]{1,0:T(8,128)S(1)}, f32[16,16]{1,0:T(8,128)S(1)}, s32[]{:T(128)}, /*index=5*/s32[]{:T(128)}) while((s32[]{:T(128)}, f32[16,16]{1,0:T(8,128)S(1)}, f32[16,16]{1,0:T(8,128)S(1)}, f32[16,16]{1,0:T(8,128)S(1)}, s32[]{:T(128)}, /*index=5*/s32[]{:T(128)}) %tuple.305), condition=%wide.region_19.20_spmd.clone, body=%wide.region_14.19_spmd.clone.sunk | while | flops 2626 | bytes 5984 | solution.py:43
  586.5 24.8 %while.130 = (s32[]{:T(128)}, f32[16,16]{1,0:T(8,128)S(1)}, f32[16,16]{1,0:T(8,128)S(1)}, f32[16,16]{1,0:T(8,128)S(1)}, s32[]{:T(128)}, /*index=5*/s32[]{:T(128)}, s32[]{:T(128)}) while((s32[]{:T(128)}, f32[16,16]{1,0:T(8,128)S(1)}, f32[16,16]{1,0:T(8,128)S(1)}, f32[16,16]{1,0:T(8,128)S(1)}, s32[]{:T(128)}, ...), condition=%wide.region_25.26_spmd.clone, body=%wide.region_20.25_spmd.clone.sunk | while | flops 2627 | bytes 6004 | solution.py:59
  611.6 21.8 %all_gather.15 = f32[16,8192]{1,0:T(8,128)S(1)} all-gather(f32[16,512]{1,0:T(8,128)S(1)} %convolution_subtract_fusion), channel_id=1, replica_groups=mesh['row'=16,'col'=16] {'row'}, dimensions={1}, use_global_device_ids=true | all-gather | bytes 557056 | tf_op jit(solution)/shard_map/all_gather | solution.py:137
  633.5 3.8 convolution_multiply_fusion.1
  637.4 5.2 scatter_fusion.1
  642.6 0.8 copy_bitcast_fusion.3
  643.5 32.5 %all_gather.14 = f32[16,8192]{1,0:T(8,128)S(1)} all-gather(f32[16,512]{1,0:T(8,128)S(1)} %convolution_subtract_fusion), channel_id=1, replica_groups=mesh['row'=16,'col'=16] {'col'}, dimensions={1}, use_global_device_ids=true | all-gather | bytes 557056 | tf_op jit(solution)/shard_map/all_gather | solution.py:136
  676.0 0.8 gather_fusion.1
  676.8 5.2 fusion.49
  682.0 0.8 copy.70
  683.5 147.0 %reduce-scatter.11.cloned.1.call-done = f32[16,512]{1,0:T(8,128)} async-done(((f32[16,8192]{1,0:T(8,128)}), f32[16,512]{1,0:T(8,128)}) %reduce-scatter.11.cloned.1.call-update) | async-done | bytes 32784 | tf_op jit(solution)/shard_map/reduce_scatter | solution.py:144
  830.5 65.7 %reduce-scatter.9.cloned.1.call-done = f32[16,512]{1,0:T(8,128)} async-done(((f32[16,8192]{1,0:T(8,128)}), f32[16,512]{1,0:T(8,128)}) %reduce-scatter.9.cloned.1.call-update) | async-done | bytes 32784 | tf_op jit(solution)/shard_map/reduce_scatter | solution.py:142
  896.2 0.9 fusion.58
  897.2 79.4 %all-reduce = (f32[48,48]{0,1:T(8,128)S(1)}, f32[48,48]{1,0:T(8,128)S(1)}) all-reduce(f32[48,48]{0,1:T(8,128)S(1)} %pad_maximum_fusion.1, f32[48,48]{1,0:T(8,128)S(1)} %fusion.70), channel_id=1, replica_groups=mesh['row'=16,'col'=16] {'row','col'}, use_global_device_ids=true, to_apply=%region_37.38 | all-reduce | flops 4608 | bytes 36864 | tf_op jit(solution)/shard_map/psum | solution.py:147
  976.8 111.3 %while.136 = (s32[]{:T(128)}, f32[48,48]{1,0:T(8,128)S(1)}, f32[48,48]{1,0:T(8,128)S(1)}, s32[]{:T(128)}, s32[]{:T(128)}) while((s32[]{:T(128)}, f32[48,48]{1,0:T(8,128)S(1)}, f32[48,48]{1,0:T(8,128)S(1)}, s32[]{:T(128)}, s32[]{:T(128)}) %tuple.311), condition=%wide.region_33.34_spmd.clone.clone, body=%wide.region_27.33_spmd.clone.clone.sunk | while | flops 25826 | bytes 48693 | solution.py:28
  1088.0 79.4 %while.131 = (s32[]{:T(128)}, f32[48,48]{1,0:T(8,128)S(1)}, f32[48,48]{1,0:T(8,128)S(1)}, f32[48,48]{1,0:T(8,128)S(1)}, s32[]{:T(128)}, /*index=5*/s32[]{:T(128)}) while((s32[]{:T(128)}, f32[48,48]{1,0:T(8,128)S(1)}, f32[48,48]{1,0:T(8,128)S(1)}, f32[48,48]{1,0:T(8,128)S(1)}, s32[]{:T(128)}, /*index=5*/s32[]{:T(128)}) %tuple.314), condition=%wide.region_43.44_spmd.clone, body=%wide.region_38.43_spmd.clone.sunk | while | flops 23234 | bytes 48480 | solution.py:43
  1092.2 0.7 subtract_divide_fusion.14
  1093.9 0.7 subtract_divide_fusion.14
  1103.8 0.7 subtract_divide_fusion.14
  1113.7 0.7 subtract_divide_fusion.14
  1115.4 0.7 subtract_divide_fusion.14
  1123.7 0.7 subtract_divide_fusion.14
  1167.5 79.4 %while.132 = (s32[]{:T(128)}, f32[48,48]{1,0:T(8,128)S(1)}, f32[48,48]{1,0:T(8,128)S(1)}, f32[48,48]{1,0:T(8,128)S(1)}, s32[]{:T(128)}, /*index=5*/s32[]{:T(128)}) while((s32[]{:T(128)}, f32[48,48]{1,0:T(8,128)S(1)}, f32[48,48]{1,0:T(8,128)S(1)}, f32[48,48]{1,0:T(8,128)S(1)}, s32[]{:T(128)}, /*index=5*/s32[]{:T(128)}) %tuple.344), condition=%wide.region_49.50_spmd.clone, body=%wide.region_44.49_spmd.clone.sunk | while | flops 23234 | bytes 48480 | solution.py:43
  1247.2 81.8 %while.133 = (s32[]{:T(128)}, f32[48,16]{0,1:T(8,128)S(1)}, f32[48,16]{0,1:T(8,128)S(1)}, f32[48,48]{1,0:T(8,128)S(1)}, s32[]{:T(128)}, /*index=5*/s32[]{:T(128)}, s32[]{:T(128)}) while((s32[]{:T(128)}, f32[48,16]{0,1:T(8,128)S(1)}, f32[48,16]{0,1:T(8,128)S(1)}, f32[48,48]{1,0:T(8,128)S(1)}, s32[]{:T(128)}, ...), condition=%wide.region_55.56_spmd.clone, body=%wide.region_50.55_spmd.clone.sunk | while | flops 10947 | bytes 23348 | solution.py:59
  1329.3 73.6 %psum.55 = f32[16,16]{1,0:T(8,128)S(1)} all-reduce(f32[16,16]{1,0:T(8,128)S(1)} %fusion.73), channel_id=1, replica_groups=mesh['row'=16,'col'=16] {'row','col'}, use_global_device_ids=true, to_apply=%region_56.57 | all-reduce | flops 256 | bytes 2048 | tf_op jit(solution)/shard_map/psum | solution.py:157
  1402.9 37.0 %while.137 = (s32[]{:T(128)}, f32[16,16]{1,0:T(8,128)S(1)}, f32[16,16]{1,0:T(8,128)S(1)}, s32[]{:T(128)}, s32[]{:T(128)}) while((s32[]{:T(128)}, f32[16,16]{1,0:T(8,128)S(1)}, f32[16,16]{1,0:T(8,128)S(1)}, s32[]{:T(128)}, s32[]{:T(128)}) %tuple.323), condition=%wide.region_63.64_spmd.clone.clone, body=%wide.region_57.63_spmd.clone.clone.sunk | while | flops 2978 | bytes 6069 | solution.py:28
  1439.9 26.3 %while.134 = (s32[]{:T(128)}, f32[16,512]{1,0:T(8,128)S(1)}, f32[16,512]{1,0:T(8,128)S(1)}, f32[16,16]{1,0:T(8,128)S(1)}, s32[]{:T(128)}, /*index=5*/s32[]{:T(128)}) while((s32[]{:T(128)}, f32[16,512]{1,0:T(8,128)S(1)}, f32[16,512]{1,0:T(8,128)S(1)}, f32[16,16]{1,0:T(8,128)S(1)}, s32[]{:T(128)}, /*index=5*/s32[]{:T(128)}) %tuple.326), condition=%wide.region_69.70_spmd.clone, body=%wide.region_64.69_spmd.clone.sunk | while | flops 66114 | bytes 144928 | solution.py:43
  (1683 shorter events, 394.3 us)
Async XLA Ops:
  7.2 41.9 %all-gather.5.cloned.1.call-start = ((), (), s32[]{:S(2)}) async-start(), calls=%async_computation.6 | async-start | bytes 1114112 | tf_op jit(solution)/shard_map/all_gather | solution.py:119
  8.7 0.6 copy-start.4
  9.4 117.1 %all-gather.3.cloned.1.call-start = ((), (), s32[]{:S(2)}) async-start(), calls=%async_computation.4 | async-start | bytes 1114112 | tf_op jit(solution)/shard_map/all_gather | solution.py:118
  10.1 318.2 %reduce-scatter.7.cloned.1.call-start = ((), (), s32[]{:S(2)}) async-start(), calls=%async_computation.7 | async-start | bytes 1114112 | tf_op jit(solution)/shard_map/reduce_scatter | solution.py:124
  61.7 333.0 %reduce-scatter.5.cloned.1.call-start = ((), (), s32[]{:S(2)}) async-start(), calls=%async_computation.5 | async-start | bytes 1114112 | tf_op jit(solution)/shard_map/reduce_scatter | solution.py:122
  134.6 1.2 copy-start.1
  135.7 694.8 %reduce-scatter.11.cloned.1.call-start = ((), (), s32[]{:S(2)}) async-start(), calls=%async_computation.9 | async-start | bytes 557056 | tf_op jit(solution)/shard_map/reduce_scatter | solution.py:144
  611.6 717.4 %copy-start.2 = (f32[16,512]{1,0:T(8,128)}, f32[16,512]{1,0:T(8,128)S(1)}, u32[]{:S(2)}) copy-start(f32[16,512]{1,0:T(8,128)S(1)} %convolution_subtract_fusion) | copy-start | bytes 98308
  643.4 252.8 %reduce-scatter.9.cloned.1.call-start = ((), (), s32[]{:S(2)}) async-start(), calls=%async_computation.8 | async-start | bytes 557056 | tf_op jit(solution)/shard_map/reduce_scatter | solution.py:142
  676.8 6.1 copy-start.3
  1247.0 219.9 %copy-start = (f32[48,48]{1,0:T(8,128)}, f32[48,48]{1,0:T(8,128)S(1)}, u32[]{:S(2)}) copy-start(f32[48,48]{1,0:T(8,128)S(1)} %get-tuple-element.811) | copy-start | bytes 27652
Sparse Core Ops, SparseCore 0:
  9.8 39.1 all-gather.4
  51.6 74.7 all-gather.2
  130.3 198.0 reduce-scatter.6
  330.7 63.9 reduce-scatter.4
  643.5 186.9 reduce-scatter.10
  832.9 63.3 reduce-scatter.8
